TPU v7x, 32 devices: a whole 2x2x4 slice. The times are simulated.
32 devices in a mesh: expert: 16 (over z, y, x), etp: 2 (over core).
Axes of the slice: x: 2, y: 2, z: 4, core: 2. Of those that a mesh axis runs over, the one named last changes fastest.
Arguments:
- grad_out: bfloat16 [2048, 3584], P('expert', 'etp'), may hold values from -6 to 6
- combine: bfloat16 [2048, 8], P('expert'), may hold values from 0.099609375 to 2.5
- expert_ids: int32 [2048, 8], P('expert'), may hold values from 0 to 31, all different within a row; in each aligned block of 128 rows (0 to 127, 128 to 255, ...) at most 64 rows name the same one
- saved_gate: bfloat16 [1024, 32, 1024], P(None, 'expert', 'etp'), may hold values from -6 to 6
- saved_up: bfloat16 [1024, 32, 1024], P(None, 'expert', 'etp'), may hold values from -1.5 to 1.5
- gate_weight: bfloat16 [32, 3584, 1024], P('expert', None, 'etp'), may hold values from -0.09375 to 0.09375
- up_weight: bfloat16 [32, 3584, 1024], P('expert', None, 'etp'), may hold values from -0.09375 to 0.09375
- down_weight: bfloat16 [32, 1024, 3584], P('expert', 'etp'), may hold values from -0.09375 to 0.09375
Outputs:
- grad_tokens: bfloat16 [2048, 3584], P('expert', 'etp')
- grad_combine: bfloat16 [2048, 8], P('expert')
Inputs may be any that keep to these rules, and one draw needn't show every extreme that they name: `expert_ids`: each token names 8 different experts. Among the 128 tokens of one block (one index of expert), at most 64 name any one expert, and some blocks reach that bound.
All inputs are finite; a program needn't handle non-finite values.
Results may differ from a plain program's by a relative error of at most 0.012.
Values may be sent and summed in bfloat16 or wider, within the bound.
A program may use at most 192 MiB of HBM per device.

v0:
```python
import jax
import jax.numpy as jnp
from jax import lax
from jax.sharding import PartitionSpec as P


def on_device(
    grad_out, combine, expert_ids, saved_gate, saved_up, gate_weight, up_weight, down_weight
):
    groups = lax.axis_size("expert")
    per_group = gate_weight.shape[0]
    tokens = grad_out.shape[0]
    capacity = saved_gate.shape[0] // groups
    hidden = saved_gate.shape[2]
    experts = groups * per_group
    chosen = expert_ids[:, :, None] == jnp.arange(experts, dtype=jnp.int32)[None, None, :]
    weights = jnp.sum(jnp.where(chosen, combine[:, :, None].astype(jnp.float32), 0.0), axis=1)
    weights = weights.astype(jnp.bfloat16).reshape(tokens, groups, per_group)
    weights = lax.all_to_all(
        weights.transpose(1, 2, 0), "expert", split_axis=0, concat_axis=0, tiled=True
    )
    rows = lax.all_gather(grad_out, "expert", axis=0, tiled=True)
    rows = lax.all_gather(rows, "etp", axis=1, tiled=True)
    rows = rows.reshape(groups, tokens, -1)
    named = (weights > 0).astype(jnp.float32)
    position = jnp.cumsum(named, axis=2) - named
    slot = jnp.where(named > 0, position, -1.0)
    select = slot[:, :, None, :] == jnp.arange(capacity, dtype=jnp.float32)[None, None, :, None]
    scale = jnp.sum(jnp.where(select, weights[:, :, None, :].astype(jnp.float32), 0.0), axis=3)
    scale = scale.transpose(1, 0, 2)[..., None]
    select = select.astype(jnp.bfloat16)
    slot_rows = jnp.einsum("blct,btd->lbcd", select, rows, preferred_element_type=jnp.bfloat16)
    grad_hidden = jnp.einsum(
        "lbcd,lfd->lbcf", slot_rows, down_weight, preferred_element_type=jnp.float32
    )
    gate_value = saved_gate.reshape(groups, capacity, per_group, hidden).transpose(2, 0, 1, 3)
    up_value = saved_up.reshape(groups, capacity, per_group, hidden).transpose(2, 0, 1, 3)
    gate_value = gate_value.astype(jnp.float32)
    up_value = up_value.astype(jnp.float32)
    gate_sigmoid = jax.nn.sigmoid(gate_value)
    activated = gate_value * gate_sigmoid
    weight_part = jnp.sum(grad_hidden * activated * up_value, axis=3)
    scaled = scale * grad_hidden
    grad_gate = (
        scaled * up_value * gate_sigmoid * (1.0 + gate_value * (1.0 - gate_sigmoid))
    ).astype(jnp.bfloat16)
    grad_up = (scaled * activated).astype(jnp.bfloat16)
    weight_tok = jnp.einsum(
        "blct,lbc->blt",
        select,
        weight_part.astype(jnp.bfloat16),
        preferred_element_type=jnp.float32,
    ).astype(jnp.bfloat16)
    weight_tok = lax.psum(weight_tok, "etp")
    weight_tok = lax.all_to_all(weight_tok, "expert", split_axis=0, concat_axis=0, tiled=True)
    weight_tok = weight_tok.transpose(2, 0, 1).reshape(tokens, 1, experts)
    grad_combine = jnp.sum(jnp.where(chosen, weight_tok.astype(jnp.float32), 0.0), axis=2).astype(
        jnp.bfloat16
    )
    partial = jnp.einsum(
        "lbcf,ldf->lbcd", grad_gate, gate_weight, preferred_element_type=jnp.float32
    )
    partial = partial + jnp.einsum(
        "lbcf,ldf->lbcd", grad_up, up_weight, preferred_element_type=jnp.float32
    )
    partial = jnp.einsum(
        "blct,lbcd->btd", select, partial.astype(jnp.bfloat16), preferred_element_type=jnp.float32
    ).astype(jnp.bfloat16)
    partial = partial.reshape(groups * tokens, -1)
    partial = lax.psum_scatter(partial, "etp", scatter_dimension=1, tiled=True)
    grad_tokens = lax.psum_scatter(partial, "expert", scatter_dimension=0, tiled=True)
    return (grad_tokens, grad_combine)


def solution(mesh):
    in_specs = (
        P("expert", "etp"),
        P("expert", None),
        P("expert", None),
        P(None, "expert", "etp"),
        P(None, "expert", "etp"),
        P("expert", None, "etp"),
        P("expert", None, "etp"),
        P("expert", "etp", None),
    )
    out_specs = (P("expert", "etp"), P("expert", None))
    return jax.shard_map(
        on_device, mesh=mesh, in_specs=in_specs, out_specs=out_specs, check_vma=False
    )
```

profile of v0, /device:TPU:10, one launch (start us, length us, event | category | flops | bytes accessed | tf_op | source)
XLA Modules:
  0.0 413.3 jit_solution(12846402701796683711)
XLA Ops:
  7.2 0.0 copy-start.3
  7.2 0.0 copy-start.2
  7.2 0.0 copy-start
  7.2 0.0 all-gather.3.cloned.1.call-start
  7.2 0.7 all-gather.3.cloned.1.call-update
  7.9 0.0 all-gather.5.cloned.1.call-start
  8.0 106.1 %all-gather.3.cloned.1.call-done = bf16[2048,1792]{1,0:T(8,128)(2,1)} async-done(((bf16[128,1792]{1,0:T(8,128)(2,1)}), bf16[2048,1792]{1,0:T(8,128)(2,1)}) %all-gather.3.cloned.1.call-update) | async-done | bytes 7340048 | tf_op jit(solution)/shard_map/all_gather | solution.py:22
  114.0 0.0 all-gather.5.cloned.1.call-update
  114.1 0.0 copy-done.3
  114.1 0.0 copy-done.2
  114.1 0.6 select_reduce_fusion.2
  114.7 5.0 %all-to-all-start = ((bf16[16,2,128]{2,1,0:T(2,128)(2,1)}), bf16[16,2,128]{2,1,0:T(2,128)(2,1)S(1)}, u32[]{:S(2)}, u32[]{:S(2)}) async-start(bf16[16,2,128]{2,1,0:T(2,128)(2,1)} %bitcast.1), calls=%async_computation | async-start | bytes 16384 | tf_op jit(solution)/shard_map/all_to_all | solution.py:19
  119.7 0.0 reduce-scatter.3.cloned.1.call-start
  119.8 0.0 copy-done
  119.8 3.1 copy.40
  122.9 0.0 copy-start.1
  122.9 4.2 %convert_element_type.97 = f32[1024,2,512]{2,1,0:T(2,128)} convert(bf16[1024,2,512]{2,1,0:T(2,128)(2,1)S(1)} %copy-done) | non-fusion elementwise | flops 1048576 | bytes 6291456 | tf_op jit(solution)/shard_map/convert_element_type | solution.py:38
  127.1 0.0 copy-done.1
  127.1 2.9 copy.39
  130.0 3.9 convert_element_type.96
  133.9 0.0 all-to-all-done
  133.9 0.8 reduce_window_sum.11
  134.7 0.4 select_reduce_fusion
  135.1 6.8 %all-gather.5.cloned.1.call-done = bf16[2048,3584]{1,0:T(8,128)(2,1)} async-done(((bf16[2048,1792]{1,0:T(8,128)(2,1)}), bf16[2048,3584]{1,0:T(8,128)(2,1)}) %all-gather.5.cloned.1.call-update) | async-done | bytes 14680080 | tf_op jit(solution)/shard_map/all_gather | solution.py:23
  141.9 21.5 %multiply_convert_fusion = (bf16[2,16,64,512]{3,2,1,0:T(8,128)(2,1)}, bf16[2,16,64,512]{3,2,1,0:T(8,128)(2,1)}, bf16[2,16,64]{2,1,0:T(8,128)(2,1)S(1)}) fusion(f32[2,16,64]{2,1,0:T(8,128)S(1)} %copy.37, f32[1024,2,512]{2,1,0:T(2,128)} %convert_element_type.97, f32[1024,2,512]{2,1,0:T(2,128)} %convert_element_type.96, f32[2,16,64,512]{3,2,1,0:T(8,128)} %bitcast.49, ...), kind=kOutput, calls=%fused_computation.12 | convolution fusion | flops 9417521152 | bytes 43020288 | tf_op jit(solution)/shard_map/lbcd,lfd->lbcf/dot_general | solution.py:33
  163.4 0.0 copy-start.4
  163.4 16.4 %fusion.6 = f32[2,16,64,3584]{3,2,0,1:T(8,128)} fusion(bf16[2,3584,512]{2,1,0:T(8,128)(2,1)} %param.14, bf16[2,16,64,512]{3,2,1,0:T(8,128)(2,1)} %get-tuple-element.2), kind=kOutput, calls=%fused_computation.7 | convolution fusion | flops 7516192768 | bytes 38797312 | tf_op jit(solution)/shard_map/lbcf,ldf->lbcd/dot_general | solution.py:63
  179.8 0.0 copy-done.4
  179.8 16.6 %fusion.8 = f32[2,16,64,3584]{3,2,0,1:T(8,128)} fusion(bf16[2,3584,512]{2,1,0:T(8,128)(2,1)} %param.13, bf16[2,16,64,512]{3,2,1,0:T(8,128)(2,1)S(1)} %copy-done.4), kind=kOutput, calls=%fused_computation.9 | convolution fusion | flops 7516192768 | bytes 38797312 | tf_op jit(solution)/shard_map/lbcf,ldf->lbcd/dot_general | solution.py:60
  196.4 25.0 %bitcast_convert_fusion = bf16[16,128,3584]{2,1,0:T(8,128)(2,1)} fusion(f32[2,16,64,3584]{3,2,0,1:T(8,128)} %fusion.8, f32[2,16,64,3584]{3,2,0,1:T(8,128)} %fusion.6, f32[16,2,128]{2,1,0:T(2,128)S(1)} %copy.36), kind=kOutput, calls=%fused_computation | convolution fusion | flops 1901330432 | bytes 73416704 | tf_op jit(solution)/shard_map/blct,lbcd->btd/dot_general | solution.py:66
  221.4 0.0 reduce-scatter.3.cloned.1.call-update
  221.4 0.0 reduce-scatter.5.cloned.1.call-start
  221.5 22.3 %reduce-scatter.3.cloned.1.call-done = bf16[2048,1792]{1,0:T(8,128)(2,1)} async-done(((bf16[2048,3584]{1,0:T(8,128)(2,1)}), bf16[2048,1792]{1,0:T(8,128)(2,1)}) %reduce-scatter.3.cloned.1.call-update) | async-done | bytes 7340048 | tf_op jit(solution)/shard_map/reduce_scatter | solution.py:70
  243.8 0.0 reduce-scatter.5.cloned.1.call-update
  243.8 0.3 fusion.15
  244.1 2.5 psum.7
  246.6 11.8 %all_to_all.10 = bf16[16,2,128]{2,1,0:T(2,128)(2,1)S(1)} all-to-all(bf16[16,2,128]{2,1,0:T(2,128)(2,1)S(1)} %psum.7), channel_id=1, replica_groups=mesh['expert'=16,'etp'=2] {'expert'}, dimensions={0} | all-to-all | bytes 16384 | tf_op jit(solution)/shard_map/all_to_all | solution.py:55
  258.4 0.6 select_reduce_fusion.1
  259.1 147.7 %reduce-scatter.5.cloned.1.call-done = bf16[128,1792]{1,0:T(8,128)(2,1)} async-done(((bf16[2048,1792]{1,0:T(8,128)(2,1)}), bf16[128,1792]{1,0:T(8,128)(2,1)}) %reduce-scatter.5.cloned.1.call-update) | async-done | bytes 458768 | tf_op jit(solution)/shard_map/reduce_scatter | solution.py:71
  (8 shorter events, 0.1 us)
Async XLA Ops:
  7.2 106.9 %copy-start.3 = (bf16[128,8]{0,1:T(8,128)(2,1)S(1)}, bf16[128,8]{0,1:T(8,128)(2,1)}, u32[]{:S(2)}) copy-start(bf16[128,8]{0,1:T(8,128)(2,1)} %param.9) | copy-start | bytes 6148
  7.2 106.9 %copy-start.2 = (s32[128,8]{0,1:T(8,128)S(1)}, s32[128,8]{0,1:T(8,128)}, u32[]{:S(2)}) copy-start(s32[128,8]{0,1:T(8,128)} %param.10) | copy-start | bytes 12292
  7.2 112.6 %copy-start = (bf16[1024,2,512]{2,1,0:T(2,128)(2,1)S(1)}, bf16[1024,2,512]{2,1,0:T(2,128)(2,1)}, u32[]{:S(2)}) copy-start(bf16[1024,2,512]{2,1,0:T(2,128)(2,1)} %param.11) | copy-start | bytes 6291460
  7.2 106.8 %all-gather.3.cloned.1.call-start = ((), (), s32[]{:S(2)}) async-start(), calls=%async_computation.4 | async-start | bytes 7798784 | tf_op jit(solution)/shard_map/all_gather | solution.py:22
  7.9 134.0 %all-gather.5.cloned.1.call-start = ((), (), s32[]{:S(2)}) async-start(), calls=%async_computation.5 | async-start | bytes 22020096 | tf_op jit(solution)/shard_map/all_gather | solution.py:23
  114.7 19.2 %all-to-all-start = ((bf16[16,2,128]{2,1,0:T(2,128)(2,1)}), bf16[16,2,128]{2,1,0:T(2,128)(2,1)S(1)}, u32[]{:S(2)}, u32[]{:S(2)}) async-start(bf16[16,2,128]{2,1,0:T(2,128)(2,1)} %bitcast.1), calls=%async_computation | async-start | bytes 16384 | tf_op jit(solution)/shard_map/all_to_all | solution.py:19
  119.7 124.0 %reduce-scatter.3.cloned.1.call-start = ((), (), s32[]{:S(2)}) async-start(), calls=%async_computation.6 | async-start | bytes 22020096 | tf_op jit(solution)/shard_map/reduce_scatter | solution.py:70
  122.9 4.2 %copy-start.1 = (bf16[1024,2,512]{2,1,0:T(2,128)(2,1)S(1)}, bf16[1024,2,512]{2,1,0:T(2,128)(2,1)}, u32[]{:S(2)}) copy-start(bf16[1024,2,512]{2,1,0:T(2,128)(2,1)} %param.12) | copy-start | bytes 6291460
  163.4 16.4 %copy-start.4 = (bf16[2,16,64,512]{3,2,1,0:T(8,128)(2,1)S(1)}, bf16[2,16,64,512]{3,2,1,0:T(8,128)(2,1)}, u32[]{:S(2)}) copy-start(bf16[2,16,64,512]{3,2,1,0:T(8,128)(2,1)} %get-tuple-element.3) | copy-start | bytes 6291460
  221.4 185.3 %reduce-scatter.5.cloned.1.call-start = ((), (), s32[]{:S(2)}) async-start(), calls=%async_computation.7 | async-start | bytes 7798784 | tf_op jit(solution)/shard_map/reduce_scatter | solution.py:71
Sparse Core Ops, SparseCore 0:
  10.7 103.3 all-gather.2
  115.6 26.2 all-gather.4
  221.5 22.2 reduce-scatter.2
  246.5 160.1 reduce-scatter.4
where the time goes:
time: 414 us; the launch traced here: 413 us
  waiting for transfers between devices  284 us (69%)
  matrix products  79.8 us (19%)
  blocking collectives  14.3 us (3%)
  between operations  13.9 us (3%)
  other arithmetic  10.5 us (3%)
  local copies, waits for them, and re-layouts  6.03 us (1%)
  starting transfers between devices  5.19 us (1%)
    reduce_scatter x1, waiting for transfers between devices, on_device(): lax.psum_scatter(partial, 'expert', scatter_dimension=0, tiled=True)  148 us
    all_gather x1, waiting for transfers between devices, on_device(): rows = lax.all_gather(grad_out, 'expert', axis=0, tiled=True)  106 us
    dot_general x1, matrix products, on_device(): jnp.einsum('blct,lbcd->btd', select, partial.astype(jnp.bfloat16), prefer...  25 us
    reduce_scatter x1, waiting for transfers between devices, on_device(): partial = lax.psum_scatter(partial, 'etp', scatter_dimension=1, tiled=True)  22.3 us
    dot_general x1, matrix products, on_device(): jnp.einsum('lbcd,lfd->lbcf', slot_rows, down_weight, preferred_element_ty...  21.5 us
    dot_general x1, matrix products, on_device(): jnp.einsum('lbcf,ldf->lbcd', grad_gate, gate_weight, preferred_element_ty...  16.6 us
    dot_general x1, matrix products, on_device(): jnp.einsum('lbcf,ldf->lbcd', grad_up, up_weight, preferred_element_type=j...  16.4 us
    all_to_all x1, blocking collectives, on_device(): lax.all_to_all(weight_tok, 'expert', split_axis=0, concat_axis=0, tiled=T...  11.8 us
  transfers between devices with their start and end apart: 5, of which 4 were waited for; matrix products, arithmetic and copies ran while one was open for 4% of the time, Pallas kernels for 0%

commit v1 on v0

--- a/solution.py
+++ b/solution.py
@@ -19,7 +19,9 @@
     weights = lax.all_to_all(
         weights.transpose(1, 2, 0), "expert", split_axis=0, concat_axis=0, tiled=True
     )
-    rows = lax.all_gather(grad_out, "expert", axis=0, tiled=True)
+    rows = jnp.concatenate(
+        lax.all_to_all(jnp.stack([grad_out] * lax.axis_size("expert")), "expert", 0, 0), axis=0
+    )
     rows = lax.all_gather(rows, "etp", axis=1, tiled=True)
     rows = rows.reshape(groups, tokens, -1)
     named = (weights > 0).astype(jnp.float32)

time: 414 us -> 474 us (1.14)
  blocking collectives: 14.3 us -> 181 us
  waiting for transfers between devices: 284 us -> 175 us
    all_to_all x0 -> x1, blocking collectives: none -> 167 us  [on_device(): lax.all_to_all(jnp.stack([grad_out] * lax.axis_size('expert')), 'expert',...]
    all_gather x1 -> x0, waiting for transfers between devices: 106 us -> none  [on_device(): rows = lax.all_gather(grad_out, 'expert', axis=0, tiled=True)]
  transfers between devices with their start and end apart: 5 -> 4, of which waited for: 4 -> 3; matrix products, arithmetic and copies ran while one was open for 4% -> 3% of each run, Pallas kernels for 0% -> 0%
where the time goes in v1:
time: 474 us
  blocking collectives  181 us (38%)
  waiting for transfers between devices  175 us (37%)
  matrix products  79.8 us (17%)
  between operations  13.8 us (3%)
  other arithmetic  9.78 us (2%)
  local copies, waits for them, and re-layouts  8.92 us (2%)
  starting transfers between devices  5.58 us (1%)
    all_to_all x1, blocking collectives, on_device(): lax.all_to_all(jnp.stack([grad_out] * lax.axis_size('expert')), 'expert',...  167 us
    reduce_scatter x1, waiting for transfers between devices, on_device(): lax.psum_scatter(partial, 'expert', scatter_dimension=0, tiled=True)  148 us
    dot_general x1, matrix products, on_device(): jnp.einsum('blct,lbcd->btd', select, partial.astype(jnp.bfloat16), prefer...  25 us
    reduce_scatter x1, waiting for transfers between devices, on_device(): partial = lax.psum_scatter(partial, 'etp', scatter_dimension=1, tiled=True)  22.3 us
    dot_general x1, matrix products, on_device(): jnp.einsum('lbcd,lfd->lbcf', slot_rows, down_weight, preferred_element_ty...  21.5 us
    dot_general x1, matrix products, on_device(): jnp.einsum('lbcf,ldf->lbcd', grad_gate, gate_weight, preferred_element_ty...  16.6 us
    dot_general x1, matrix products, on_device(): jnp.einsum('lbcf,ldf->lbcd', grad_up, up_weight, preferred_element_type=j...  16.4 us
    all_to_all x1, blocking collectives, on_device(): lax.all_to_all(weight_tok, 'expert', split_axis=0, concat_axis=0, tiled=T...  11.8 us
  transfers between devices with their start and end apart: 4, of which 3 were waited for; matrix products, arithmetic and copies ran while one was open for 3% of the time, Pallas kernels for 0%

profile of v1, /device:TPU:10, one launch (start us, length us, event | category | flops | bytes accessed | tf_op | source)
XLA Modules:
  0.0 474.1 jit_solution(7451369004410705761)
XLA Ops:
  7.2 0.0 all-gather.2.cloned.1.call-start
  7.2 1.7 stack.2
  8.9 166.7 %all_to_all.15 = bf16[16,128,1792]{2,1,0:T(8,128)(2,1)} all-to-all(bf16[16,128,1792]{2,1,0:T(8,128)(2,1)S(1)} %stack.2), channel_id=1, replica_groups=mesh['expert'=16,'etp'=2] {'expert'}, dimensions={0} | all-to-all | bytes 14680064 | tf_op jit(solution)/shard_map/all_to_all | solution.py:23
  175.7 0.0 copy-start.3
  175.7 0.0 copy-start.2
  175.7 0.0 copy-start
  175.7 0.0 all-gather.2.cloned.1.call-update
  175.7 0.7 copy-done.3
  176.4 0.0 copy-done.2
  176.4 0.6 select_reduce_fusion.2
  177.0 5.5 %all-to-all-start = ((bf16[16,2,128]{2,1,0:T(2,128)(2,1)}), bf16[16,2,128]{2,1,0:T(2,128)(2,1)S(1)}, u32[]{:S(2)}, u32[]{:S(2)}) async-start(bf16[16,2,128]{2,1,0:T(2,128)(2,1)} %bitcast.1), calls=%async_computation | async-start | bytes 16384 | tf_op jit(solution)/shard_map/all_to_all | solution.py:19
  182.5 0.0 reduce-scatter.3.cloned.1.call-start
  182.5 0.0 copy-done
  182.5 3.6 copy.40
  186.1 0.0 copy-start.1
  186.1 3.8 convert_element_type.97
  189.9 0.0 copy-done.1
  189.9 2.9 copy.39
  192.9 3.5 convert_element_type.96
  196.4 0.0 all-to-all-done
  196.4 0.8 reduce_window_sum.11
  197.2 0.4 select_reduce_fusion
  197.6 5.0 %all-gather.2.cloned.1.call-done = bf16[2048,3584]{1,0:T(8,128)(2,1)} async-done(((bf16[2048,1792]{1,0:T(8,128)(2,1)}), bf16[2048,3584]{1,0:T(8,128)(2,1)}) %all-gather.2.cloned.1.call-update) | async-done | bytes 14680080 | tf_op jit(solution)/shard_map/all_gather | solution.py:25
  202.6 21.5 %multiply_convert_fusion = (bf16[2,16,64,512]{3,2,1,0:T(8,128)(2,1)}, bf16[2,16,64,512]{3,2,1,0:T(8,128)(2,1)}, bf16[2,16,64]{2,1,0:T(8,128)(2,1)S(1)}) fusion(f32[2,16,64]{2,1,0:T(8,128)S(1)} %copy.37, f32[1024,2,512]{2,1,0:T(2,128)} %convert_element_type.97, f32[1024,2,512]{2,1,0:T(2,128)} %convert_element_type.96, f32[2,16,64,512]{3,2,1,0:T(8,128)} %bitcast.51, ...), kind=kOutput, calls=%fused_computation.12 | convolution fusion | flops 9417521152 | bytes 43020288 | tf_op jit(solution)/shard_map/lbcd,lfd->lbcf/dot_general | solution.py:35
  224.1 0.0 copy-start.4
  224.1 16.4 %fusion.6 = f32[2,16,64,3584]{3,2,0,1:T(8,128)} fusion(bf16[2,3584,512]{2,1,0:T(8,128)(2,1)} %param.14, bf16[2,16,64,512]{3,2,1,0:T(8,128)(2,1)} %get-tuple-element.2), kind=kOutput, calls=%fused_computation.7 | convolution fusion | flops 7516192768 | bytes 38797312 | tf_op jit(solution)/shard_map/lbcf,ldf->lbcd/dot_general | solution.py:65
  240.4 0.0 copy-done.4
  240.4 16.6 %fusion.8 = f32[2,16,64,3584]{3,2,0,1:T(8,128)} fusion(bf16[2,3584,512]{2,1,0:T(8,128)(2,1)} %param.13, bf16[2,16,64,512]{3,2,1,0:T(8,128)(2,1)S(1)} %copy-done.4), kind=kOutput, calls=%fused_computation.9 | convolution fusion | flops 7516192768 | bytes 38797312 | tf_op jit(solution)/shard_map/lbcf,ldf->lbcd/dot_general | solution.py:62
  257.0 25.0 %bitcast_convert_fusion = bf16[16,128,3584]{2,1,0:T(8,128)(2,1)} fusion(f32[2,16,64,3584]{3,2,0,1:T(8,128)} %fusion.8, f32[2,16,64,3584]{3,2,0,1:T(8,128)} %fusion.6, f32[16,2,128]{2,1,0:T(2,128)S(1)} %copy.36), kind=kOutput, calls=%fused_computation | convolution fusion | flops 1901330432 | bytes 73416704 | tf_op jit(solution)/shard_map/blct,lbcd->btd/dot_general | solution.py:68
  282.1 0.0 reduce-scatter.3.cloned.1.call-update
  282.1 0.0 reduce-scatter.5.cloned.1.call-start
  282.1 22.3 %reduce-scatter.3.cloned.1.call-done = bf16[2048,1792]{1,0:T(8,128)(2,1)} async-done(((bf16[2048,3584]{1,0:T(8,128)(2,1)}), bf16[2048,1792]{1,0:T(8,128)(2,1)}) %reduce-scatter.3.cloned.1.call-update) | async-done | bytes 7340048 | tf_op jit(solution)/shard_map/reduce_scatter | solution.py:72
  304.5 0.0 reduce-scatter.5.cloned.1.call-update
  304.5 0.3 fusion.15
  304.8 2.5 psum.7
  307.3 11.8 %all_to_all.16 = bf16[16,2,128]{2,1,0:T(2,128)(2,1)S(1)} all-to-all(bf16[16,2,128]{2,1,0:T(2,128)(2,1)S(1)} %psum.7), channel_id=1, replica_groups=mesh['expert'=16,'etp'=2] {'expert'}, dimensions={0} | all-to-all | bytes 16384 | tf_op jit(solution)/shard_map/all_to_all | solution.py:57
  319.1 0.6 select_reduce_fusion.1
  319.7 147.8 %reduce-scatter.5.cloned.1.call-done = bf16[128,1792]{1,0:T(8,128)(2,1)} async-done(((bf16[2048,1792]{1,0:T(8,128)(2,1)}), bf16[128,1792]{1,0:T(8,128)(2,1)}) %reduce-scatter.5.cloned.1.call-update) | async-done | bytes 458768 | tf_op jit(solution)/shard_map/reduce_scatter | solution.py:73
  (8 shorter events, 0.1 us)
Async XLA Ops:
  7.2 195.4 %all-gather.2.cloned.1.call-start = ((), (), s32[]{:S(2)}) async-start(), calls=%async_computation.5 | async-start | bytes 22020096 | tf_op jit(solution)/shard_map/all_gather | solution.py:25
  175.7 0.7 copy-start.3
  175.7 0.7 copy-start.2
  175.7 6.8 %copy-start = (bf16[1024,2,512]{2,1,0:T(2,128)(2,1)S(1)}, bf16[1024,2,512]{2,1,0:T(2,128)(2,1)}, u32[]{:S(2)}) copy-start(bf16[1024,2,512]{2,1,0:T(2,128)(2,1)} %param.11) | copy-start | bytes 6291460
  177.0 19.4 %all-to-all-start = ((bf16[16,2,128]{2,1,0:T(2,128)(2,1)}), bf16[16,2,128]{2,1,0:T(2,128)(2,1)S(1)}, u32[]{:S(2)}, u32[]{:S(2)}) async-start(bf16[16,2,128]{2,1,0:T(2,128)(2,1)} %bitcast.1), calls=%async_computation | async-start | bytes 16384 | tf_op jit(solution)/shard_map/all_to_all | solution.py:19
  182.5 122.0 %reduce-scatter.3.cloned.1.call-start = ((), (), s32[]{:S(2)}) async-start(), calls=%async_computation.6 | async-start | bytes 22020096 | tf_op jit(solution)/shard_map/reduce_scatter | solution.py:72
  186.1 3.9 copy-start.1
  224.1 16.4 %copy-start.4 = (bf16[2,16,64,512]{3,2,1,0:T(8,128)(2,1)S(1)}, bf16[2,16,64,512]{3,2,1,0:T(8,128)(2,1)}, u32[]{:S(2)}) copy-start(bf16[2,16,64,512]{3,2,1,0:T(8,128)(2,1)} %get-tuple-element.3) | copy-start | bytes 6291460
  282.1 185.5 %reduce-scatter.5.cloned.1.call-start = ((), (), s32[]{:S(2)}) async-start(), calls=%async_computation.7 | async-start | bytes 7798784 | tf_op jit(solution)/shard_map/reduce_scatter | solution.py:73
Sparse Core Ops, SparseCore 0:
  175.8 26.6 all-gather.1
  282.2 22.2 reduce-scatter.2
  307.3 160.1 reduce-scatter.4
